TPU v7x, 512 devices: a whole 4x8x8 slice. The times are simulated.
512 devices in a mesh: wide: 64 (over z, y_hi, core), narrow: 8 (over y_lo, x).
Axes of the slice: x: 4, y: 8 (y_hi: 4, y_lo: 2; y = y_hi * 2 + y_lo), z: 8, core: 2. Of those that a mesh axis runs over, the one named last changes fastest.
Arguments:
- tile_values: bfloat16 [3584, 512, 512], P(('wide', 'narrow')), may hold values from -0.25 to 0.25
- tile_row: int32 [3584], P(('wide', 'narrow')), may hold values from 0 to 1
- tile_col: int32 [3584], P(('wide', 'narrow')), may hold values from 0 to 7
- basis: float32 [524288, 256], P(('wide', 'narrow')), may hold values from -6 to 6
Outputs:
- next_basis: float32 [4096, 256], P('wide')
All inputs are finite; a program needn't handle non-finite values.
Results may differ from a plain program's by a relative error of at most 0.0032.
Values sent between devices are 32-bit elements; how exact they have to be, the bound alone decides.
No kernel may reach another device: no remote copies, remote signals or barrier semaphores. Data moves between devices by JAX's collectives and lax.ppermute only.
A program may use at most 64 MiB of HBM per device.

v0:
```python
import jax
import jax.numpy as jnp
from jax import lax
from jax.sharding import PartitionSpec as P

COLS_DEV = 64


def finish(owned_rows, gram_sum):
    factor = jnp.linalg.cholesky(gram_sum)
    return jax.scipy.linalg.solve_triangular(factor, owned_rows.T, lower=True).T


def gram_terms(owned_rows):
    return jnp.dot(
        owned_rows.T,
        owned_rows,
        precision=lax.Precision.HIGHEST,
        preferred_element_type=jnp.float32,
    )


def body(tile_values, tile_row, tile_col, basis):
    tile_edge = tile_values.shape[1]
    basis_width = basis.shape[1]
    blocks = basis.astype(jnp.bfloat16).reshape(basis.shape[0] // tile_edge, tile_edge, basis_width)
    chosen = jnp.take(blocks, tile_row, axis=0)
    products = jnp.einsum("tij,tik->tjk", tile_values, chosen, preferred_element_type=jnp.float32)
    col_blocks = COLS_DEV * lax.axis_size("wide") // tile_edge
    one_hot = (tile_col[None, :] == jnp.arange(col_blocks, dtype=jnp.int32)[:, None]).astype(
        jnp.float32
    )
    partial_value = jnp.einsum("ct,tjk->cjk", one_hot, products, precision=lax.Precision.HIGHEST)
    total_rows = col_blocks * tile_edge
    partial_value = partial_value.reshape(total_rows, basis_width)
    reduced = lax.psum_scatter(partial_value, "wide", scatter_dimension=0, tiled=True)
    owned_rows = lax.psum(reduced, "narrow")
    gram_sum = lax.psum(gram_terms(owned_rows), "wide") / total_rows
    return finish(owned_rows, gram_sum)


def solution(mesh):
    in_specs = (
        P(("wide", "narrow"), None, None),
        P(("wide", "narrow")),
        P(("wide", "narrow")),
        P(("wide", "narrow"), None),
    )
    out_specs = P("wide", None)
    return jax.shard_map(body, mesh=mesh, in_specs=in_specs, out_specs=out_specs, check_vma=False)
```

profile of v0, /device:TPU:1, one launch (start us, length us, event | category | flops | bytes accessed | tf_op | source)
XLA Modules:
  0.0 864.6 jit_solution(9576807460728252653)
XLA Ops:
  6.5 0.0 reduce-scatter.2.cloned.1.call-start
  6.5 0.7 compare_select_fusion
  7.2 0.7 compare_and_fusion
  7.9 1.3 convert_element_type.4
  9.2 0.7 gather_fusion
  9.8 5.1 fusion.2
  15.0 0.0 copy-start.1
  15.0 5.3 copy.10
  20.2 0.0 copy-done.1
  20.2 4.2 fusion
  24.5 3.2 copy.7
  27.7 0.0 reduce-scatter.2.cloned.1.call-update
  27.7 0.0 all-reduce.4.cloned.1.call-start
  27.7 157.9 %reduce-scatter.2.cloned.1.call-done = f32[64,256]{1,0:T(8,128)} async-done(((f32[4096,256]{1,0:T(8,128)}), f32[64,256]{1,0:T(8,128)}) %reduce-scatter.2.cloned.1.call-update) | async-done | bytes 65552 | tf_op jit(solution)/shard_map/reduce_scatter | solution.py:36
  185.6 0.0 all-reduce.4.cloned.1.call-update
  185.6 0.2 all-reduce.6.cloned.1.call-start
  185.9 83.3 %all-reduce.4.cloned.1.call-done = f32[64,256]{1,0:T(8,128)} async-done(((f32[64,256]{1,0:T(8,128)}), f32[64,256]{1,0:T(8,128)}) %all-reduce.4.cloned.1.call-update) | async-done | bytes 65552 | tf_op jit(solution)/shard_map/psum | solution.py:37
  269.2 0.0 copy-start
  269.2 2.1 fusion.19
  271.2 0.0 all-reduce.6.cloned.1.call-update
  271.3 523.6 %all-reduce.6.cloned.1.call-done = f32[256,256]{0,1:T(8,128)} async-done(((f32[256,256]{0,1:T(8,128)}), f32[256,256]{0,1:T(8,128)}) %all-reduce.6.cloned.1.call-update) | async-done | bytes 262160 | tf_op jit(solution)/shard_map/psum | solution.py:38
  794.8 1.0 broadcast_multiply_fusion
  795.8 0.1 copy.9
  796.0 1.0 fusion.6
  797.0 11.7 %cholesky.50 = f32[128,128]{1,0:T(8,128)S(1)} custom-call(f32[128,128]{1,0:T(8,128)S(1)} %cholesky.118), custom_call_target="Cholesky" | custom-call | tf_op jit(solution)/shard_map/jit(cholesky)/cholesky | solution.py:10
  808.7 9.8 %custom-call.15 = f32[1,128,128]{1,2,0:T(8,128)S(1)} custom-call(f32[1,128,128]{2,1,0:T(8,128)S(1)} %get-tuple-element.26), custom_call_target="InvertDiagBlocksLowerTriangular" | custom-call | tf_op jit(solution)/shard_map/jit(cholesky)/cholesky | solution.py:10
  818.5 0.2 constant_dynamic-update-slice_fusion.1
  818.8 0.3 convolution_subtract_fusion
  819.0 11.7 %cholesky.105 = f32[128,128]{1,0:T(8,128)S(1)} custom-call(f32[128,128]{1,0:T(8,128)S(1)} %convolution_subtract_fusion), custom_call_target="Cholesky" | custom-call | tf_op jit(solution)/shard_map/jit(cholesky)/cholesky | solution.py:10
  830.8 0.7 compare_reduce_fusion
  832.8 0.1 triangular_solve.57
  832.9 4.2 while.1
  833.1 0.7 fusion.28
  833.7 1.3 bitcast_dynamic-update-slice_fusion.2
  835.1 0.7 fusion.28
  835.8 1.3 bitcast_dynamic-update-slice_fusion.2
  837.1 19.7 %custom-call.16 = f32[2,128,128]{1,2,0:T(8,128)S(1)} custom-call(f32[2,128,128]{2,1,0:T(8,128)S(1)} %get-tuple-element.12), custom_call_target="InvertDiagBlocksLowerTriangular" | custom-call | tf_op jit(solution)/shard_map/jit(_solve_triangular)/triangular_solve | solution.py:11
  856.8 0.0 copy-done
  856.8 0.2 fusion.9
  857.0 0.2 convolution_subtract_fusion.1
  857.2 0.2 fusion.8
  857.4 0.6 maximum_bitcast_fusion
  (10 shorter events, 0.2 us)
Async XLA Ops:
  6.5 179.1 %reduce-scatter.2.cloned.1.call-start = ((), (), s32[]{:S(2)}) async-start(), calls=%async_computation.1 | async-start | bytes 4259840 | tf_op jit(solution)/shard_map/reduce_scatter | solution.py:36
  15.0 5.3 copy-start.1
  27.7 241.5 %all-reduce.4.cloned.1.call-start = ((), (), s32[]{:S(2)}) async-start(), calls=%async_computation.2 | async-start | bytes 131072 | tf_op jit(solution)/shard_map/psum | solution.py:37
  185.6 609.2 %all-reduce.6.cloned.1.call-start = ((), (), s32[]{:S(2)}) async-start(), calls=%async_computation.3 | async-start | bytes 524288 | tf_op jit(solution)/shard_map/psum | solution.py:38
  269.2 587.6 %copy-start = (f32[64,256]{1,0:T(8,128)S(1)}, f32[64,256]{1,0:T(8,128)}, u32[]{:S(2)}) copy-start(f32[64,256]{1,0:T(8,128)} %all-reduce.4.cloned.1.call-done) | copy-start | bytes 196612
Sparse Core Ops, SparseCore 0:
  27.8 157.7 reduce-scatter.1
  188.5 80.6 all-reduce.3
  272.1 522.7 all-reduce.5
where the time goes:
time: 865 us
  waiting for transfers between devices  765 us (88%)
  other arithmetic  58.9 us (7%)
  between operations  14.5 us (2%)
  local copies, waits for them, and re-layouts  13.4 us (2%)
  matrix products  12.5 us (1%)
    psum x1, waiting for transfers between devices, body(): gram_sum = lax.psum(gram_terms(owned_rows), 'wide') / total_rows  524 us
    reduce_scatter x1, waiting for transfers between devices, body(): lax.psum_scatter(partial_value, 'wide', scatter_dimension=0, tiled=True)  158 us
    psum x1, waiting for transfers between devices, body(): owned_rows = lax.psum(reduced, 'narrow')  83.3 us
    another operation x6, other arithmetic, finish(): factor = jnp.linalg.cholesky(gram_sum)  34 us
    another operation x3, other arithmetic, finish(): return jax.scipy.linalg.solve_triangular(factor, owned_rows.T, lower=True).T  19.7 us
  transfers between devices with their start and end apart: 3, of which 3 were waited for; matrix products, arithmetic and copies ran while one was open for 0% of the time, Pallas kernels for 0%

commit v1 on v0

--- a/solution.py
+++ b/solution.py
@@ -4,6 +4,11 @@
 from jax.sharding import PartitionSpec as P
 
 COLS_DEV = 64
+
+
+def summed_here(shard, name):
+    parts = lax.all_gather(shard, name)
+    return jnp.sum(parts, axis=0)
 
 
 def finish(owned_rows, gram_sum):
@@ -35,7 +40,7 @@
     partial_value = partial_value.reshape(total_rows, basis_width)
     reduced = lax.psum_scatter(partial_value, "wide", scatter_dimension=0, tiled=True)
     owned_rows = lax.psum(reduced, "narrow")
-    gram_sum = lax.psum(gram_terms(owned_rows), "wide") / total_rows
+    gram_sum = summed_here(gram_terms(owned_rows), "wide") / total_rows
     return finish(owned_rows, gram_sum)
 
 

time: 865 us -> 493 us (0.57)
  waiting for transfers between devices: 765 us -> 387 us
    psum x1 -> x0, waiting for transfers between devices: 524 us -> none  [body(): gram_sum = lax.psum(gram_terms(owned_rows), 'wide') / total_rows]
    all_gather x0 -> x1, waiting for transfers between devices: none -> 146 us  [summed_here(): parts = lax.all_gather(shard, name)]
where the time goes in v1:
time: 493 us; the launch traced here: 492 us
  waiting for transfers between devices  387 us (78%)
  other arithmetic  63.9 us (13%)
  between operations  14.5 us (3%)
  local copies, waits for them, and re-layouts  13.4 us (3%)
  matrix products  12.5 us (3%)
    reduce_scatter x1, waiting for transfers between devices, body(): lax.psum_scatter(partial_value, 'wide', scatter_dimension=0, tiled=True)  158 us
    all_gather x1, waiting for transfers between devices, summed_here(): parts = lax.all_gather(shard, name)  146 us
    psum x1, waiting for transfers between devices, body(): owned_rows = lax.psum(reduced, 'narrow')  83.3 us
    another operation x6, other arithmetic, finish(): factor = jnp.linalg.cholesky(gram_sum)  34 us
    another operation x3, other arithmetic, finish(): return jax.scipy.linalg.solve_triangular(factor, owned_rows.T, lower=True).T  19.7 us
  transfers between devices with their start and end apart: 3, of which 3 were waited for; matrix products, arithmetic and copies ran while one was open for 0% of the time, Pallas kernels for 0%

profile of v1, /device:TPU:1, one launch (start us, length us, event | category | flops | bytes accessed | tf_op | source)
XLA Modules:
  0.0 492.2 jit_solution(11907528115673163367)
XLA Ops:
  6.5 0.0 reduce-scatter.2.cloned.1.call-start
  6.5 0.7 compare_select_fusion
  7.2 0.7 compare_and_fusion
  7.9 1.3 convert_element_type.4
  9.2 0.7 gather_fusion
  9.8 5.1 %convolution_bitcast_fusion = f32[7,512,256]{1,2,0:T(8,128)} fusion(bf16[7,512,512]{2,1,0:T(8,128)(2,1)} %param.4, bf16[7,512,256]{2,1,0:T(8,128)(2,1)S(1)} %gather_fusion, pred[7]{0:T(512)(128)(4,1)S(1)} %compare_and_fusion), kind=kOutput, calls=%fused_computation.3 | convolution fusion | flops 940441600 | bytes 9175047 | tf_op jit(solution)/shard_map/tij,tik->tjk/dot_general | solution.py:33
  15.0 0.0 copy-start.1
  15.0 5.3 %copy.12 = f32[7,512,256]{2,0,1:T(8,128)} copy(f32[7,512,256]{1,2,0:T(8,128)} %convolution_bitcast_fusion) | data formatting | bytes 7340032 | tf_op jit(solution)/shard_map/tij,tik->tjk/dot_general | solution.py:33
  20.2 0.0 copy-done.1
  20.2 4.2 fusion.12
  24.5 3.2 copy.13
  27.7 0.0 reduce-scatter.2.cloned.1.call-update
  27.7 0.0 all-reduce.3.cloned.1.call-start
  27.7 157.9 %reduce-scatter.2.cloned.1.call-done = f32[64,256]{1,0:T(8,128)} async-done(((f32[4096,256]{1,0:T(8,128)}), f32[64,256]{1,0:T(8,128)}) %reduce-scatter.2.cloned.1.call-update) | async-done | bytes 65552 | tf_op jit(solution)/shard_map/reduce_scatter | solution.py:41
  185.6 0.0 all-reduce.3.cloned.1.call-update
  185.6 0.2 all-gather.3.cloned.1.call-start
  185.9 83.3 %all-reduce.3.cloned.1.call-done = f32[64,256]{1,0:T(8,128)} async-done(((f32[64,256]{1,0:T(8,128)}), f32[64,256]{1,0:T(8,128)}) %all-reduce.3.cloned.1.call-update) | async-done | bytes 65552 | tf_op jit(solution)/shard_map/psum | solution.py:42
  269.2 2.0 fusion.17
  271.2 0.0 all-gather.3.cloned.1.call-update
  271.2 146.2 %all-gather.3.cloned.1.call-done = f32[16384,256]{1,0:T(8,128)} async-done(((f32[256,256]{1,0:T(8,128)}), f32[16384,256]{1,0:T(8,128)}) %all-gather.3.cloned.1.call-update) | async-done | bytes 16777232 | tf_op jit(solution)/shard_map/all_gather | solution.py:10
  417.5 6.8 %reduce_sum.11 = f32[256,256]{1,0:T(8,128)S(1)} reduce(f32[64,256,256]{2,1,0:T(8,128)} %bitcast.46, f32[]{:T(128)} %constant.94.clone.1), dimensions={0}, to_apply=%region_2.3 | reduce | flops 4128768 | bytes 17039364 | tf_op jit(solution)/shard_map/reduce_sum | solution.py:11
  424.3 0.0 copy-start
  424.3 0.1 copy.14
  424.5 11.7 %cholesky.50 = f32[128,128]{1,0:T(8,128)S(1)} custom-call(f32[128,128]{1,0:T(8,128)S(1)} %cholesky.118), custom_call_target="Cholesky" | custom-call | tf_op jit(solution)/shard_map/jit(cholesky)/cholesky | solution.py:15
  436.3 9.8 %custom-call.15 = f32[1,128,128]{1,2,0:T(8,128)S(1)} custom-call(f32[1,128,128]{2,1,0:T(8,128)S(1)} %get-tuple-element.26), custom_call_target="InvertDiagBlocksLowerTriangular" | custom-call | tf_op jit(solution)/shard_map/jit(cholesky)/cholesky | solution.py:15
  446.1 0.2 constant_dynamic-update-slice_fusion.1
  446.3 0.3 convolution_subtract_fusion
  446.6 11.7 %cholesky.105 = f32[128,128]{1,0:T(8,128)S(1)} custom-call(f32[128,128]{1,0:T(8,128)S(1)} %convolution_subtract_fusion), custom_call_target="Cholesky" | custom-call | tf_op jit(solution)/shard_map/jit(cholesky)/cholesky | solution.py:15
  458.3 0.7 compare_reduce_fusion
  460.4 0.1 triangular_solve.57
  460.4 4.2 while.1
  460.6 0.7 fusion.27
  461.3 1.3 bitcast_dynamic-update-slice_fusion.2
  462.7 0.7 fusion.27
  463.3 1.3 bitcast_dynamic-update-slice_fusion.2
  464.7 19.7 %custom-call.16 = f32[2,128,128]{1,2,0:T(8,128)S(1)} custom-call(f32[2,128,128]{2,1,0:T(8,128)S(1)} %get-tuple-element.12), custom_call_target="InvertDiagBlocksLowerTriangular" | custom-call | tf_op jit(solution)/shard_map/jit(_solve_triangular)/triangular_solve | solution.py:16
  484.4 0.0 copy-done
  484.4 0.2 fusion.6
  484.6 0.2 convolution_subtract_fusion.1
  484.8 0.2 fusion.5
  485.0 0.6 maximum_bitcast_fusion
  (11 shorter events, 0.2 us)
Async XLA Ops:
  6.5 179.1 %reduce-scatter.2.cloned.1.call-start = ((), (), s32[]{:S(2)}) async-start(), calls=%async_computation.1 | async-start | bytes 4259840 | tf_op jit(solution)/shard_map/reduce_scatter | solution.py:41
  15.0 5.3 %copy-start.1 = (s32[7]{0:T(128)S(1)}, s32[7]{0:T(128)}, u32[]{:S(2)}) copy-start(s32[7]{0:T(128)} %param.6) | copy-start | bytes 88
  27.7 241.5 %all-reduce.3.cloned.1.call-start = ((), (), s32[]{:S(2)}) async-start(), calls=%async_computation.2 | async-start | bytes 131072 | tf_op jit(solution)/shard_map/psum | solution.py:42
  185.6 231.9 %all-gather.3.cloned.1.call-start = ((), (), s32[]{:S(2)}) async-start(), calls=%async_computation.3 | async-start | bytes 17039360 | tf_op jit(solution)/shard_map/all_gather | solution.py:10
  424.3 60.0 %copy-start = (f32[64,256]{1,0:T(8,128)S(1)}, f32[64,256]{1,0:T(8,128)}, u32[]{:S(2)}) copy-start(f32[64,256]{1,0:T(8,128)} %all-reduce.3.cloned.1.call-done) | copy-start | bytes 196612
Sparse Core Ops, SparseCore 0:
  27.8 157.7 reduce-scatter.1
  188.5 80.6 all-reduce.2
  272.5 144.9 all-gather.2
